TPU v7x, 32 devices: a whole 2x2x4 slice. The times are simulated.
32 devices in a mesh: row: 8 (over y, x, core), col: 4 (over z).
Axes of the slice: x: 2, y: 2, z: 4, core: 2. Of those that a mesh axis runs over, the one named last changes fastest.
Arguments:
- blocks: bfloat16 [8, 4, 320, 128, 128], P('row', 'col'), may hold values from -0.1875 to 0.1875
- block_rows: int32 [8, 4, 320], P('row', 'col'), may hold values from 0 to 1023, as said below
- block_cols: int32 [8, 4, 320], P('row', 'col'), may hold values from 0 to 1023, as said below
- counts: int32 [8, 4], P('row', 'col'), may hold values from 160 to 320, as said below
- panel: bfloat16 [32, 131072], P(None, ('row', 'col'))
Outputs:
- basis: bfloat16 [32, 131072], P(None, ('row', 'col'))
- factor: float32 [32, 32], replicated
Inputs may be any that keep to these rules, and one draw needn't show every extreme that they name: `block_rows`: split the block-rows into shards of 32 in order; every block of device (r, c) lies in a block-row of a shard whose index modulo 4 is c. Pairs may repeat. `block_cols`: every block of device (r, c) lies in a block-column of a shard whose index divided by 4 is r. `counts`: some device has all 320 slots live.
All inputs are finite; a program needn't handle non-finite values.
Results may differ from a plain program's by a relative error of at most 0.001.
Values may be sent and summed in bfloat16 or wider, within the bound.
No kernel may reach another device: no remote copies, remote signals or barrier semaphores. Data moves between devices by JAX's collectives and lax.ppermute only.
A program may use at most 64 MiB of HBM per device.

v0:
```python
import jax
import jax.numpy as jnp
from jax import lax
from jax.sharding import PartitionSpec as P


def on_device(blocks, block_rows, block_cols, counts, panel):
    width = blocks.shape[-1]
    slot_count = blocks.shape[2]
    panel_cols = panel.shape[0]
    nb_dev = panel.shape[1] // width
    grid_rows = lax.axis_size("row")
    grid_cols = lax.axis_size("col")
    span = nb_dev * grid_cols
    whole = lax.all_gather(panel, "col", axis=1, tiled=True)
    tiles = whole.reshape(panel_cols, span, width)
    global_rows = block_rows[0, 0]
    local_cols = block_cols[0, 0] % span
    local_rows = global_rows // span * nb_dev + global_rows % nb_dev
    live = (jnp.arange(slot_count, dtype=jnp.int32) < counts[0, 0]).astype(jnp.float32)
    picked = jnp.take(tiles, local_cols, axis=1)
    products = jnp.einsum("psk,sjk->spj", picked, blocks[0, 0], preferred_element_type=jnp.float32)
    products = products * live[:, None, None]
    partial_sum = jax.ops.segment_sum(products, local_rows, num_segments=grid_rows * nb_dev)
    owned = lax.psum_scatter(partial_sum, "row", scatter_dimension=0, tiled=True)
    product_t = jnp.transpose(owned, (1, 0, 2)).reshape(panel_cols, nb_dev * width)
    total_rows = nb_dev * width * grid_rows * grid_cols
    local_gram = jnp.dot(
        product_t, product_t.T, precision=lax.Precision.HIGHEST, preferred_element_type=jnp.float32
    )
    gram = lax.psum(local_gram, ("row", "col")) / total_rows
    lower = jnp.linalg.cholesky(gram)
    basis = jax.scipy.linalg.solve_triangular(lower, product_t, lower=True)
    return (basis.astype(jnp.bfloat16), lower.T)


def solution(mesh):
    in_specs = (
        P("row", "col", None, None, None),
        P("row", "col", None),
        P("row", "col", None),
        P("row", "col"),
        P(None, ("row", "col")),
    )
    out_specs = (P(None, ("row", "col")), P())
    return jax.shard_map(
        on_device, mesh=mesh, in_specs=in_specs, out_specs=out_specs, check_vma=False
    )
```

profile of v0, /device:TPU:0, one launch (start us, length us, event | category | flops | bytes accessed | tf_op | source)
XLA Modules:
  0.0 211.6 jit_solution(440297915687399267)
XLA Ops:
  7.2 0.0 all-gather.2.cloned.1.call-start
  7.2 0.7 all-gather.2.cloned.1.call-update
  7.9 0.0 reduce-scatter.2.cloned.1.call-start
  8.6 0.7 reduce.7
  9.3 0.7 fusion.19
  10.0 0.7 fusion.21
  10.7 29.5 %all-gather.2.cloned.1.call-done = bf16[32,16384]{1,0:T(8,128)(2,1)} async-done(((bf16[32,4096]{1,0:T(8,128)(2,1)}), bf16[32,16384]{1,0:T(8,128)(2,1)}) %all-gather.2.cloned.1.call-update) | async-done | bytes 1048592 | tf_op jit(solution)/shard_map/all_gather | solution.py:15
  40.2 1.4 copy_bitcast_fusion
  41.6 3.0 %gather_fusion = bf16[320,32,128]{2,1,0:T(8,128)(2,1)} fusion(bf16[32,128,128]{2,0,1:T(8,128)(2,1)S(1)} %copy_bitcast_fusion, s32[1024]{0:T(1024)S(1)} %pad_clamp_fusion), kind=kCustom, calls=%fused_computation | custom fusion | bytes 5244160 | tf_op jit(solution)/shard_map/jit(_take)/gather | solution.py:21
  44.7 12.7 %broadcast_multiply_fusion = f32[320,32,128]{2,1,0:T(8,128)} fusion(f32[320]{0:T(512)S(1)} %get-tuple-element.10, bf16[1,1,320,128,128]{4,3,2,1,0:T(8,128)(2,1)} %param.5, bf16[320,32,128]{2,1,0:T(8,128)(2,1)} %gather_fusion, pred[320]{0:T(512)(128)(4,1)S(1)} %get-tuple-element.11), kind=kOutput, calls=%fused_computation.7 | convolution fusion | flops 338165760 | bytes 18351680 | tf_op jit(solution)/shard_map/psk,sjk->spj/dot_general | solution.py:22
  57.4 2.5 %broadcast_in_dim.17 = f32[256,32,128]{2,1,0:T(8,128)} broadcast(f32[]{:T(128)} %constant.88.clone.1), dimensions={} | broadcast | bytes 4194308 | tf_op jit(solution)/shard_map/broadcast_in_dim | solution.py:24
  59.9 42.8 %scatter_fusion = f32[256,32,128]{2,1,0:T(8,128)} fusion(f32[256,32,128]{2,1,0:T(8,128)} %broadcast_in_dim.17, s32[320]{0:T(512)S(1)} %fusion.21, f32[320,32,128]{2,1,0:T(8,128)} %broadcast_multiply_fusion), kind=kCustom, calls=%fused_computation.1 | custom fusion | flops 1310720 | bytes 15729920 | tf_op jit(solution)/shard_map/scatter-add | solution.py:24
  102.7 0.0 reduce-scatter.2.cloned.1.call-update
  102.7 51.0 %reduce-scatter.2.cloned.1.call-done = f32[32,32,128]{2,1,0:T(8,128)} async-done(((f32[256,32,128]{2,1,0:T(8,128)}), f32[32,32,128]{2,1,0:T(8,128)}) %reduce-scatter.2.cloned.1.call-update) | async-done | bytes 524304 | tf_op jit(solution)/shard_map/reduce_scatter | solution.py:25
  153.7 1.8 convolution_bitcast_fusion
  155.5 39.4 %psum.7 = f32[32,32]{0,1:T(8,128)S(1)} all-reduce(f32[32,32]{0,1:T(8,128)S(1)} %convolution_bitcast_fusion), channel_id=1, replica_groups=mesh['row'=8,'col'=4] {'row','col'}, use_global_device_ids=true, to_apply=%region_2.3 | all-reduce | flops 1024 | bytes 8192 | tf_op jit(solution)/shard_map/psum | solution.py:31
  194.9 0.1 copy.17
  195.0 2.9 %cholesky.16 = f32[32,32]{1,0:T(8,128)S(1)} custom-call(f32[32,32]{1,0:T(8,128)S(1)} %fusion.14), custom_call_target="Cholesky" | custom-call | tf_op jit(solution)/shard_map/jit(cholesky)/cholesky | solution.py:32
  198.0 0.6 compare_reduce_fusion
  198.6 0.7 fusion.15
  199.3 0.7 copy.19
  199.9 2.4 %custom-call.7 = f32[1,32,32]{1,2,0:T(8,128)S(1)} custom-call(f32[1,32,32]{2,1,0:T(8,128)S(1)} %get-tuple-element.9), custom_call_target="InvertDiagBlocksLowerTriangular" | custom-call | tf_op jit(solution)/shard_map/jit(_solve_triangular)/triangular_solve | solution.py:33
  202.4 2.4 %convolution_convert_fusion = bf16[32,4096]{1,0:T(8,128)(2,1)} fusion(f32[1,32,32]{1,2,0:T(8,128)S(1)} %custom-call.7, f32[32,32,128]{2,1,0:T(8,128)} %reduce-scatter.2.cloned.1.call-done), kind=kOutput, calls=%fused_computation.4 | convolution fusion | flops 50462720 | bytes 790528 | tf_op jit(solution)/shard_map/jit(_solve_triangular)/triangular_solve | solution.py:33
  (5 shorter events, 0.1 us)
Async XLA Ops:
  7.2 33.1 %all-gather.2.cloned.1.call-start = ((), (), s32[]{:S(2)}) async-start(), calls=%async_computation.1 | async-start | bytes 1310720 | tf_op jit(solution)/shard_map/all_gather | solution.py:15
  7.9 145.8 %reduce-scatter.2.cloned.1.call-start = ((), (), s32[]{:S(2)}) async-start(), calls=%async_computation.2 | async-start | bytes 4718592 | tf_op jit(solution)/shard_map/reduce_scatter | solution.py:25
Sparse Core Ops, SparseCore 0:
  9.6 30.6 all-gather.1
  102.9 50.8 reduce-scatter.1
where the time goes:
time: 212 us
  waiting for transfers between devices  81.2 us (38%)
  other arithmetic  51.6 us (24%)
  blocking collectives  39.4 us (19%)
  matrix products  16.8 us (8%)
  between operations  14.7 us (7%)
  local copies, waits for them, and re-layouts  7.72 us (4%)
    reduce_scatter x1, waiting for transfers between devices, on_device(): lax.psum_scatter(partial_sum, 'row', scatter_dimension=0, tiled=True)  51 us
    scatter-add x1, other arithmetic, on_device(): jax.ops.segment_sum(products, local_rows, num_segments=grid_rows * nb_dev)  42.8 us
    psum x1, blocking collectives, on_device(): gram = lax.psum(local_gram, ('row', 'col')) / total_rows  39.4 us
    all_gather x1, waiting for transfers between devices, on_device(): whole = lax.all_gather(panel, 'col', axis=1, tiled=True)  29.5 us
    dot_general x1, matrix products, on_device(): jnp.einsum('psk,sjk->spj', picked, blocks[0, 0], preferred_element_type=j...  12.7 us
  transfers between devices with their start and end apart: 2, of which 2 were waited for; matrix products, arithmetic and copies ran while one was open for 1% of the time, Pallas kernels for 0%

commit v1 on v0

--- a/solution.py
+++ b/solution.py
@@ -2,6 +2,27 @@
 import jax.numpy as jnp
 from jax import lax
 from jax.sharding import PartitionSpec as P
+
+
+def gather_around(shard, axis, dim):
+    devices, place, rows = (lax.axis_size(axis), lax.axis_index(axis), shard.shape[dim])
+    right = [(i, (i + 1) % devices) for i in range(devices)]
+    left = [(i, (i - 1) % devices) for i in range(devices)]
+    out = jnp.zeros((*shard.shape[:dim], devices * rows, *shard.shape[dim + 1 :]), shard.dtype)
+    out = lax.dynamic_update_slice_in_dim(out, shard, place * rows, axis=dim)
+    from_left = from_right = shard
+    half = devices // 2
+    for step in range(1, half + 1):
+        from_left = lax.ppermute(from_left, axis, right)
+        out = lax.dynamic_update_slice_in_dim(
+            out, from_left, (place - step) % devices * rows, axis=dim
+        )
+        if step < devices - half:
+            from_right = lax.ppermute(from_right, axis, left)
+            out = lax.dynamic_update_slice_in_dim(
+                out, from_right, (place + step) % devices * rows, axis=dim
+            )
+    return out
 
 
 def on_device(blocks, block_rows, block_cols, counts, panel):
@@ -12,7 +33,7 @@
     grid_rows = lax.axis_size("row")
     grid_cols = lax.axis_size("col")
     span = nb_dev * grid_cols
-    whole = lax.all_gather(panel, "col", axis=1, tiled=True)
+    whole = gather_around(panel, "col", 1)
     tiles = whole.reshape(panel_cols, span, width)
     global_rows = block_rows[0, 0]
     local_cols = block_cols[0, 0] % span

time: 212 us -> 203 us (0.958)
  waiting for transfers between devices: 81.2 us -> 65.3 us
  starting transfers between devices: 0.08 us -> 6.76 us
    all_gather x1 -> x0, waiting for transfers between devices: 29.5 us -> none  [on_device(): whole = lax.all_gather(panel, 'col', axis=1, tiled=True)]
    ppermute x0 -> x3, waiting for transfers between devices: none -> 15.6 us  [the longest x2 15.6 us: gather_around(): from_left = lax.ppermute(from_left, axis, right)]
    ppermute x0 -> x3, starting transfers between devices: none -> 6.73 us  [the longest x1 5.1 us: gather_around(): from_right = lax.ppermute(from_right, axis, left)]
  transfers between devices with their start and end apart: 2 -> 4, of which waited for: 2 -> 3; matrix products, arithmetic and copies ran while one was open for 1% -> 2% of each run, Pallas kernels for 0% -> 0%
where the time goes in v1:
time: 203 us; the launch traced here: 202 us
  waiting for transfers between devices  65.3 us (32%)
  other arithmetic  51.6 us (25%)
  blocking collectives  39.4 us (19%)
  matrix products  16.9 us (8%)
  between operations  14.8 us (7%)
  local copies, waits for them, and re-layouts  7.61 us (4%)
  starting transfers between devices  6.76 us (3%)
    reduce_scatter x1, waiting for transfers between devices, on_device(): lax.psum_scatter(partial_sum, 'row', scatter_dimension=0, tiled=True)  49.7 us
    scatter-add x1, other arithmetic, on_device(): jax.ops.segment_sum(products, local_rows, num_segments=grid_rows * nb_dev)  42.8 us
    psum x1, blocking collectives, on_device(): gram = lax.psum(local_gram, ('row', 'col')) / total_rows  39.4 us
    ppermute x2, waiting for transfers between devices, gather_around(): from_left = lax.ppermute(from_left, axis, right)  15.6 us
    dot_general x1, matrix products, on_device(): jnp.einsum('psk,sjk->spj', picked, blocks[0, 0], preferred_element_type=j...  12.7 us
    ppermute x1, starting transfers between devices, gather_around(): from_right = lax.ppermute(from_right, axis, left)  5.1 us
  transfers between devices with their start and end apart: 4, of which 3 were waited for; matrix products, arithmetic and copies ran while one was open for 2% of the time, Pallas kernels for 0%

profile of v1, /device:TPU:0, one launch (start us, length us, event | category | flops | bytes accessed | tf_op | source)
XLA Modules:
  0.0 202.4 jit_solution(2956414949260222491)
XLA Ops:
  7.2 0.0 reduce-scatter.2.cloned.1.call-start
  7.2 5.1 %collective-permute-start.1 = (bf16[32,4096]{1,0:T(8,128)(2,1)}, bf16[32,4096]{1,0:T(8,128)(2,1)S(1)}, u32[]{:S(2)}, u32[]{:S(2)}) collective-permute-start(bf16[32,4096]{1,0:T(8,128)(2,1)} %param.9), channel_id=1, source_target_pairs={{0,3},{1,0},{2,1},{3,2},{4,7},{5,4},{6,5},{7,6},{8,11},{9,8},{10,9... | collective-permute-start | bytes 786440 | tf_op jit(solution)/shard_map/ppermute | solution.py:21
  12.3 0.0 collective-permute-start
  12.3 0.7 fusion.21
  13.0 0.7 fusion.19
  13.7 0.1 broadcast_in_dim.22
  13.8 1.0 constant_dynamic-update-slice_fusion.3
  14.9 0.7 reduce.7
  16.2 8.4 %collective-permute-done = bf16[32,4096]{1,0:T(8,128)(2,1)S(1)} collective-permute-done((bf16[32,4096]{1,0:T(8,128)(2,1)}, bf16[32,4096]{1,0:T(8,128)(2,1)S(1)}, u32[]{:S(2)}, u32[]{:S(2)}) %collective-permute-start) | collective-permute-done | bytes 262176 | tf_op jit(solution)/shard_map/ppermute | solution.py:16
  24.6 1.6 collective-permute-start.2
  26.3 0.0 collective-permute-done.1
  26.3 7.3 %collective-permute-done.2 = bf16[32,4096]{1,0:T(8,128)(2,1)S(1)} collective-permute-done((bf16[32,4096]{1,0:T(8,128)(2,1)S(1)}, bf16[32,4096]{1,0:T(8,128)(2,1)S(1)}, u32[]{:S(2)}, u32[]{:S(2)}) %collective-permute-start.2) | collective-permute-done | bytes 262176 | tf_op jit(solution)/shard_map/ppermute | solution.py:16
  33.6 0.2 copy_bitcast_fusion
  33.8 3.0 %gather_fusion = bf16[320,32,128]{2,1,0:T(8,128)(2,1)} fusion(bf16[32,128,128]{2,0,1:T(8,128)(2,1)S(1)} %copy_bitcast_fusion, s32[1024]{0:T(1024)S(1)} %pad_clamp_fusion), kind=kCustom, calls=%fused_computation | custom fusion | bytes 5244160 | tf_op jit(solution)/shard_map/jit(_take)/gather | solution.py:42
  36.8 12.7 %broadcast_multiply_fusion = f32[320,32,128]{2,1,0:T(8,128)} fusion(f32[320]{0:T(512)S(1)} %get-tuple-element.10, bf16[1,1,320,128,128]{4,3,2,1,0:T(8,128)(2,1)} %param.5, bf16[320,32,128]{2,1,0:T(8,128)(2,1)} %gather_fusion, pred[320]{0:T(512)(128)(4,1)S(1)} %get-tuple-element.11), kind=kOutput, calls=%fused_computation.7 | convolution fusion | flops 338165760 | bytes 18351680 | tf_op jit(solution)/shard_map/psk,sjk->spj/dot_general | solution.py:43
  49.5 2.5 %broadcast_in_dim.20 = f32[256,32,128]{2,1,0:T(8,128)} broadcast(f32[]{:T(128)} %constant.117.clone.1), dimensions={} | broadcast | bytes 4194308 | tf_op jit(solution)/shard_map/broadcast_in_dim | solution.py:45
  52.1 42.8 %scatter_fusion = f32[256,32,128]{2,1,0:T(8,128)} fusion(f32[256,32,128]{2,1,0:T(8,128)} %broadcast_in_dim.20, s32[320]{0:T(512)S(1)} %fusion.21, f32[320,32,128]{2,1,0:T(8,128)} %broadcast_multiply_fusion), kind=kCustom, calls=%fused_computation.1 | custom fusion | flops 1310720 | bytes 15729920 | tf_op jit(solution)/shard_map/scatter-add | solution.py:45
  94.9 0.0 reduce-scatter.2.cloned.1.call-update
  94.9 49.7 %reduce-scatter.2.cloned.1.call-done = f32[32,32,128]{2,1,0:T(8,128)} async-done(((f32[256,32,128]{2,1,0:T(8,128)}), f32[32,32,128]{2,1,0:T(8,128)}) %reduce-scatter.2.cloned.1.call-update) | async-done | bytes 524304 | tf_op jit(solution)/shard_map/reduce_scatter | solution.py:46
  144.5 1.8 convolution_bitcast_fusion
  146.3 39.4 %psum.7 = f32[32,32]{0,1:T(8,128)S(1)} all-reduce(f32[32,32]{0,1:T(8,128)S(1)} %convolution_bitcast_fusion), channel_id=1, replica_groups=mesh['row'=8,'col'=4] {'row','col'}, use_global_device_ids=true, to_apply=%region_2.3 | all-reduce | flops 1024 | bytes 8192 | tf_op jit(solution)/shard_map/psum | solution.py:52
  185.7 0.1 copy.17
  185.8 2.9 %cholesky.16 = f32[32,32]{1,0:T(8,128)S(1)} custom-call(f32[32,32]{1,0:T(8,128)S(1)} %fusion.14), custom_call_target="Cholesky" | custom-call | tf_op jit(solution)/shard_map/jit(cholesky)/cholesky | solution.py:53
  188.8 0.6 compare_reduce_fusion
  189.4 0.7 fusion.15
  190.1 0.7 copy.19
  190.8 2.4 %custom-call.7 = f32[1,32,32]{1,2,0:T(8,128)S(1)} custom-call(f32[1,32,32]{2,1,0:T(8,128)S(1)} %get-tuple-element.9), custom_call_target="InvertDiagBlocksLowerTriangular" | custom-call | tf_op jit(solution)/shard_map/jit(_solve_triangular)/triangular_solve | solution.py:54
  193.2 2.4 %convolution_convert_fusion = bf16[32,4096]{1,0:T(8,128)(2,1)} fusion(f32[1,32,32]{1,2,0:T(8,128)S(1)} %custom-call.7, f32[32,32,128]{2,1,0:T(8,128)} %reduce-scatter.2.cloned.1.call-done), kind=kOutput, calls=%fused_computation.4 | convolution fusion | flops 50462720 | bytes 790528 | tf_op jit(solution)/shard_map/jit(_solve_triangular)/triangular_solve | solution.py:54
  (8 shorter events, 0.1 us)
Async XLA Ops:
  7.2 137.4 %reduce-scatter.2.cloned.1.call-start = ((), (), s32[]{:S(2)}) async-start(), calls=%async_computation.1 | async-start | bytes 4718592 | tf_op jit(solution)/shard_map/reduce_scatter | solution.py:46
  7.2 19.0 %collective-permute-start.1 = (bf16[32,4096]{1,0:T(8,128)(2,1)}, bf16[32,4096]{1,0:T(8,128)(2,1)S(1)}, u32[]{:S(2)}, u32[]{:S(2)}) collective-permute-start(bf16[32,4096]{1,0:T(8,128)(2,1)} %param.9), channel_id=1, source_target_pairs={{0,3},{1,0},{2,1},{3,2},{4,7},{5,4},{6,5},{7,6},{8,11},{9,8},{10,9... | collective-permute-start | bytes 786440 | tf_op jit(solution)/shard_map/ppermute | solution.py:21
  12.3 12.3 %collective-permute-start = (bf16[32,4096]{1,0:T(8,128)(2,1)}, bf16[32,4096]{1,0:T(8,128)(2,1)S(1)}, u32[]{:S(2)}, u32[]{:S(2)}) collective-permute-start(bf16[32,4096]{1,0:T(8,128)(2,1)} %param.9), channel_id=1, source_target_pairs={{0,1},{1,2},{2,3},{3,0},{4,5},{5,6},{6,7},{7,4},{8,9},{9,10},{10,1... | collective-permute-start | bytes 786440 | tf_op jit(solution)/shard_map/ppermute | solution.py:16
  24.6 9.0 %collective-permute-start.2 = (bf16[32,4096]{1,0:T(8,128)(2,1)S(1)}, bf16[32,4096]{1,0:T(8,128)(2,1)S(1)}, u32[]{:S(2)}, u32[]{:S(2)}) collective-permute-start(bf16[32,4096]{1,0:T(8,128)(2,1)S(1)} %collective-permute-done), channel_id=1, source_target_pairs={{0,1},{1,2},{2,3},{3,0},{4,5},{5,6},{6,7},{7,4},{8,9},{9,10},{10,1... | collective-permute-start | bytes 786440 | tf_op jit(solution)/shard_map/ppermute | solution.py:16
Sparse Core Ops, SparseCore 0:
  95.0 49.4 reduce-scatter.1

commit v2 on v0

--- a/solution.py
+++ b/solution.py
@@ -28,7 +28,7 @@
     local_gram = jnp.dot(
         product_t, product_t.T, precision=lax.Precision.HIGHEST, preferred_element_type=jnp.float32
     )
-    gram = lax.psum(local_gram, ("row", "col")) / total_rows
+    gram = jnp.sum(lax.all_gather(local_gram, ("row", "col")), axis=0) / total_rows
     lower = jnp.linalg.cholesky(gram)
     basis = jax.scipy.linalg.solve_triangular(lower, product_t, lower=True)
     return (basis.astype(jnp.bfloat16), lower.T)

time: 212 us -> 244 us (1.15)
  blocking collectives: 39.4 us -> 71.1 us
    all_gather x0 -> x1, blocking collectives: none -> 71.1 us  [on_device(): lax.all_gather(local_gram, ('row', 'col'))]
    psum x1 -> x0, blocking collectives: 39.4 us -> none  [on_device(): gram = lax.psum(local_gram, ('row', 'col')) / total_rows]
where the time goes in v2:
time: 244 us; the launch traced here: 243 us
  waiting for transfers between devices  81.2 us (33%)
  blocking collectives  71.1 us (29%)
  other arithmetic  51.7 us (21%)
  matrix products  16.9 us (7%)
  between operations  14.7 us (6%)
  local copies, waits for them, and re-layouts  7.72 us (3%)
    all_gather x1, blocking collectives, on_device(): lax.all_gather(local_gram, ('row', 'col'))  71.1 us
    reduce_scatter x1, waiting for transfers between devices, on_device(): lax.psum_scatter(partial_sum, 'row', scatter_dimension=0, tiled=True)  51 us
    scatter-add x1, other arithmetic, on_device(): jax.ops.segment_sum(products, local_rows, num_segments=grid_rows * nb_dev)  42.8 us
    all_gather x1, waiting for transfers between devices, on_device(): whole = lax.all_gather(panel, 'col', axis=1, tiled=True)  29.5 us
    dot_general x1, matrix products, on_device(): jnp.einsum('psk,sjk->spj', picked, blocks[0, 0], preferred_element_type=j...  12.7 us
  transfers between devices with their start and end apart: 2, of which 2 were waited for; matrix products, arithmetic and copies ran while one was open for 1% of the time, Pallas kernels for 0%

profile of v2, /device:TPU:0, one launch (start us, length us, event | category | flops | bytes accessed | tf_op | source)
XLA Modules:
  0.0 243.3 jit_solution(12116223484282675301)
XLA Ops:
  7.2 0.0 all-gather.3.cloned.1.call-start
  7.2 0.7 all-gather.3.cloned.1.call-update
  7.9 0.0 reduce-scatter.2.cloned.1.call-start
  8.6 0.7 reduce.7
  9.3 0.7 fusion.19
  10.0 0.7 fusion.21
  10.7 29.5 %all-gather.3.cloned.1.call-done = bf16[32,16384]{1,0:T(8,128)(2,1)} async-done(((bf16[32,4096]{1,0:T(8,128)(2,1)}), bf16[32,16384]{1,0:T(8,128)(2,1)}) %all-gather.3.cloned.1.call-update) | async-done | bytes 1048592 | tf_op jit(solution)/shard_map/all_gather | solution.py:15
  40.2 1.4 copy_bitcast_fusion
  41.6 3.0 %gather_fusion = bf16[320,32,128]{2,1,0:T(8,128)(2,1)} fusion(bf16[32,128,128]{2,0,1:T(8,128)(2,1)S(1)} %copy_bitcast_fusion, s32[1024]{0:T(1024)S(1)} %pad_clamp_fusion), kind=kCustom, calls=%fused_computation | custom fusion | bytes 5244160 | tf_op jit(solution)/shard_map/jit(_take)/gather | solution.py:21
  44.7 12.7 %broadcast_multiply_fusion = f32[320,32,128]{2,1,0:T(8,128)} fusion(f32[320]{0:T(512)S(1)} %get-tuple-element.12, bf16[1,1,320,128,128]{4,3,2,1,0:T(8,128)(2,1)} %param.5, bf16[320,32,128]{2,1,0:T(8,128)(2,1)} %gather_fusion, pred[320]{0:T(512)(128)(4,1)S(1)} %get-tuple-element.13), kind=kOutput, calls=%fused_computation.7 | convolution fusion | flops 338165760 | bytes 18351680 | tf_op jit(solution)/shard_map/psk,sjk->spj/dot_general | solution.py:22
  57.4 2.5 %broadcast_in_dim.17 = f32[256,32,128]{2,1,0:T(8,128)} broadcast(f32[]{:T(128)} %constant.90.clone.1), dimensions={} | broadcast | bytes 4194308 | tf_op jit(solution)/shard_map/broadcast_in_dim | solution.py:24
  59.9 42.8 %scatter_fusion = f32[256,32,128]{2,1,0:T(8,128)} fusion(f32[256,32,128]{2,1,0:T(8,128)} %broadcast_in_dim.17, s32[320]{0:T(512)S(1)} %fusion.21, f32[320,32,128]{2,1,0:T(8,128)} %broadcast_multiply_fusion), kind=kCustom, calls=%fused_computation.1 | custom fusion | flops 1310720 | bytes 15729920 | tf_op jit(solution)/shard_map/scatter-add | solution.py:24
  102.7 0.0 reduce-scatter.2.cloned.1.call-update
  102.7 51.0 %reduce-scatter.2.cloned.1.call-done = f32[32,32,128]{2,1,0:T(8,128)} async-done(((f32[256,32,128]{2,1,0:T(8,128)}), f32[32,32,128]{2,1,0:T(8,128)}) %reduce-scatter.2.cloned.1.call-update) | async-done | bytes 524304 | tf_op jit(solution)/shard_map/reduce_scatter | solution.py:25
  153.7 1.8 convolution_bitcast_fusion
  155.5 71.1 %all-gather = f32[1024,32]{1,0:T(8,128)S(1)} all-gather(f32[32,32]{1,0:T(8,128)S(1)} %convolution_bitcast_fusion), channel_id=2, replica_groups=mesh['row'=8,'col'=4] {'row','col'}, dimensions={0}, use_global_device_ids=true | all-gather | bytes 135168 | tf_op jit(solution)/shard_map/all_gather | solution.py:31
  226.6 0.1 reduce_sum.11
  226.7 0.1 copy.18
  226.7 2.9 %cholesky.16 = f32[32,32]{1,0:T(8,128)S(1)} custom-call(f32[32,32]{1,0:T(8,128)S(1)} %fusion.14), custom_call_target="Cholesky" | custom-call | tf_op jit(solution)/shard_map/jit(cholesky)/cholesky | solution.py:32
  229.7 0.6 compare_reduce_fusion
  230.3 0.7 fusion.15
  231.0 0.7 copy.20
  231.7 2.4 %custom-call.7 = f32[1,32,32]{1,2,0:T(8,128)S(1)} custom-call(f32[1,32,32]{2,1,0:T(8,128)S(1)} %get-tuple-element.11), custom_call_target="InvertDiagBlocksLowerTriangular" | custom-call | tf_op jit(solution)/shard_map/jit(_solve_triangular)/triangular_solve | solution.py:33
  234.1 2.4 convolution_convert_fusion
  (4 shorter events, 0.1 us)
Async XLA Ops:
  7.2 33.1 %all-gather.3.cloned.1.call-start = ((), (), s32[]{:S(2)}) async-start(), calls=%async_computation.1 | async-start | bytes 1310720 | tf_op jit(solution)/shard_map/all_gather | solution.py:15
  7.9 145.8 %reduce-scatter.2.cloned.1.call-start = ((), (), s32[]{:S(2)}) async-start(), calls=%async_computation.2 | async-start | bytes 4718592 | tf_op jit(solution)/shard_map/reduce_scatter | solution.py:25
Sparse Core Ops, SparseCore 0:
  9.6 30.6 all-gather.2
  102.9 50.8 reduce-scatter.1
